TPU v7x, 32 devices: a whole 2x2x4 slice. The times are simulated.
32 devices in a mesh: expert: 4 (over z), tensor: 8 (over y, x, core).
Axes of the slice: x: 2, y: 2, z: 4, core: 2. Of those that a mesh axis runs over, the one named last changes fastest.
Arguments:
- tokens: bfloat16 [1024, 4096], P(('expert', 'tensor')), may hold values from -6 to 6
- router: float32 [4096, 4], replicated, may hold values from -0.09375 to 0.09375
- choice_ids: int32 [1024, 2], P(('expert', 'tensor')), may hold values from 0 to 3, all different within a row; in each aligned block of 32 rows (0 to 31, 32 to 63, ...) at most 20 rows name the same one
- w_gate: bfloat16 [4, 4096, 14336], P('expert', None, 'tensor'), may hold values from -0.09375 to 0.09375
- w_up: bfloat16 [4, 4096, 14336], P('expert', None, 'tensor'), may hold values from -0.09375 to 0.09375
- w_down: bfloat16 [4, 14336, 4096], P('expert', 'tensor'), may hold values from -0.046875 to 0.046875
Outputs:
- mixed: bfloat16 [1024, 4096], P(('expert', 'tensor'))
Inputs may be any that keep to these rules, and one draw needn't show every extreme that they name: `choice_ids`: the 2 experts of a token differ. In each aligned block of 32 rows (the rows of one device) each expert is named by at most 20 rows, a bound that some block reaches.
All inputs are finite; a program needn't handle non-finite values.
Results may differ from a plain program's by a relative error of at most 0.015.
Values may be sent and summed in bfloat16 or wider, within the bound.
No kernel may reach another device: no remote copies, remote signals or barrier semaphores. Data moves between devices by JAX's collectives and lax.ppermute only.
A program may use at most 128 MiB of HBM per device.

v0:
```python
import jax
import jax.numpy as jnp
from jax import lax
from jax.sharding import PartitionSpec as P


def hidden_units(row_piece, weight_gate, weight_up):
    gate_proj = jnp.dot(row_piece, weight_gate, preferred_element_type=jnp.float32)
    up_proj = jnp.dot(row_piece, weight_up, preferred_element_type=jnp.float32)
    return (jax.nn.silu(gate_proj) * up_proj).astype(jnp.bfloat16)


def on_device(tokens, router, choice_ids, w_gate, w_up, w_down):
    tok_count, feat_width = tokens.shape
    top_count = choice_ids.shape[1]
    experts = lax.axis_size("expert")
    capacity = tok_count * top_count * 5 // (experts * 4)
    group_rows = experts * capacity
    weight_gate = w_gate[0]
    weight_up = w_up[0]
    weight_down = w_down[0]
    logits = jnp.dot(tokens.astype(jnp.float32), router, precision=lax.Precision.HIGHEST)
    picked = jnp.take_along_axis(logits, choice_ids, axis=1)
    gate_weights = jax.nn.softmax(picked, axis=1)
    flat_ids = choice_ids.reshape(-1)
    onehot = (flat_ids[:, None] == jnp.arange(experts, dtype=jnp.int32)[None, :]).astype(jnp.int32)
    slot_rank = jnp.cumsum(onehot, axis=0) - onehot
    slot_index = jnp.sum(slot_rank * onehot, axis=1)
    destination = flat_ids * capacity + slot_index
    dispatch_map = (
        jnp.arange(group_rows, dtype=jnp.int32)[:, None] == destination[None, :]
    ).astype(jnp.bfloat16)
    doubled = jnp.repeat(tokens, top_count, axis=0)
    buffer = jnp.dot(dispatch_map, doubled, preferred_element_type=jnp.float32).astype(jnp.bfloat16)
    arrived = lax.all_to_all(buffer, "expert", split_axis=0, concat_axis=0, tiled=True)
    hidden = hidden_units(
        lax.all_gather(arrived, "tensor", axis=0, tiled=True), weight_gate, weight_up
    )
    partial_value = jnp.dot(hidden, weight_down, preferred_element_type=jnp.float32)
    summed = lax.psum(partial_value.astype(jnp.bfloat16), "tensor").astype(jnp.float32)
    own_rows = lax.dynamic_slice_in_dim(
        summed, lax.axis_index("tensor") * group_rows, group_rows, 0
    )
    expert_out = own_rows.astype(jnp.bfloat16)
    returned = lax.all_to_all(expert_out, "expert", split_axis=0, concat_axis=0, tiled=True)
    gathered = jnp.dot(dispatch_map.T, returned, preferred_element_type=jnp.float32).reshape(
        tok_count, top_count, feat_width
    )
    result = jnp.sum(gathered * gate_weights[:, :, None], axis=1)
    return result.astype(jnp.bfloat16)


def solution(mesh):
    in_specs = (
        P(("expert", "tensor"), None),
        P(),
        P(("expert", "tensor"), None),
        P("expert", None, "tensor"),
        P("expert", None, "tensor"),
        P("expert", "tensor", None),
    )
    out_specs = P(("expert", "tensor"), None)
    return jax.shard_map(
        on_device, mesh=mesh, in_specs=in_specs, out_specs=out_specs, check_vma=False
    )
```

profile of v0, /device:TPU:0, one launch (start us, length us, event | category | flops | bytes accessed | tf_op | source)
XLA Modules:
  0.0 253.6 jit_solution(12875386895920183099)
XLA Ops:
  6.5 0.0 copy-start
  6.5 0.0 all-gather.2.cloned.1.call-start
  6.5 0.8 copy.26
  7.3 0.1 reshape.74
  7.4 0.1 fusion.15
  7.5 0.1 reduce_window_sum.11
  7.6 0.2 select_reduce_fusion
  7.8 0.0 copy-start.3
  7.8 1.4 broadcast_in_dim.6
  9.2 0.2 reshape.75
  9.5 0.3 convolution_convert_fusion
  9.8 0.0 copy-done.3
  9.8 0.1 all_to_all.16
  9.9 26.3 %all_to_all.24 = bf16[4,20,4096]{2,1,0:T(8,128)(2,1)S(1)} all-to-all(bf16[4,20,4096]{2,1,0:T(8,128)(2,1)S(1)} %all_to_all.16), channel_id=1, replica_groups=mesh['expert'=4,'tensor'=8] {'expert'}, dimensions={0} | all-to-all | bytes 1310720 | tf_op jit(solution)/shard_map/all_to_all | solution.py:35
  36.2 1.0 all_to_all.18
  37.2 0.0 all-gather.2.cloned.1.call-update
  37.2 0.0 all-reduce.2.cloned.1.call-start
  37.3 40.2 %all-gather.2.cloned.1.call-done = bf16[640,4096]{1,0:T(8,128)(2,1)} async-done(((bf16[80,4096]{1,0:T(8,128)(2,1)}), bf16[640,4096]{1,0:T(8,128)(2,1)}) %all-gather.2.cloned.1.call-update) | async-done | bytes 5242896 | tf_op jit(solution)/shard_map/all_gather | solution.py:37
  77.4 15.9 %fusion.4 = f32[640,1792]{1,0:T(8,128)} fusion(bf16[640,4096]{1,0:T(8,128)(2,1)} %all-gather.2.cloned.1.call-done, bf16[1,4096,1792]{2,1,0:T(8,128)(2,1)} %param.9), kind=kOutput, calls=%fused_computation.5 | convolution fusion | flops 9395240960 | bytes 24510464 | tf_op jit(solution)/shard_map/dot_general | solution.py:8
  93.3 33.1 %fusion.6 = bf16[640,4096]{1,0:T(8,128)(2,1)} fusion(bf16[1,1792,4096]{2,1,0:T(8,128)(2,1)} %param.11, f32[640,1792]{1,0:T(8,128)} %fusion.4, bf16[640,4096]{1,0:T(8,128)(2,1)} %all-gather.2.cloned.1.call-done, bf16[1,4096,1792]{2,1,0:T(8,128)(2,1)} %param.10), kind=kOutput, calls=%fused_computation.7 | convolution fusion | flops 18799984640 | bytes 44433408 | tf_op jit(solution)/shard_map/dot_general | solution.py:39
  126.5 0.0 copy-start.2
  126.5 0.0 copy-start.1
  126.5 0.0 all-reduce.2.cloned.1.call-update
  126.5 0.6 copy-done.2
  127.2 0.1 copy.28
  127.2 0.1 reshape.77
  127.4 91.7 %all-reduce.2.cloned.1.call-done = bf16[640,4096]{1,0:T(8,128)(2,1)} async-done(((bf16[640,4096]{1,0:T(8,128)(2,1)}), bf16[640,4096]{1,0:T(8,128)(2,1)}) %all-reduce.2.cloned.1.call-update) | async-done | bytes 5242896 | tf_op jit(solution)/shard_map/psum | solution.py:40
  219.0 1.1 convert_convert_fusion
  220.1 1.0 all_to_all.19
  221.2 4.6 %all-to-all-start.1 = ((bf16[4,20,4096]{2,1,0:T(8,128)(2,1)}), bf16[4,20,4096]{2,1,0:T(8,128)(2,1)S(1)}, u32[]{:S(2)}, u32[]{:S(2)}) async-start(bf16[4,20,4096]{2,1,0:T(8,128)(2,1)} %all_to_all.19), calls=%async_computation.1 | async-start | bytes 1572864 | tf_op jit(solution)/shard_map/all_to_all | solution.py:45
  225.8 0.0 copy-done
  225.8 0.0 copy-done.1
  225.8 0.3 fusion.22
  226.1 0.0 copy-start.4
  226.1 0.9 gather_fusion
  227.0 0.1 reshape.80
  227.1 0.1 copy.29
  227.2 0.0 copy-done.4
  227.2 0.1 iota_compare_fusion.3
  227.3 18.3 %all-to-all-done.1 = bf16[4,20,4096]{2,1,0:T(8,128)(2,1)S(1)} async-done(((bf16[4,20,4096]{2,1,0:T(8,128)(2,1)}), bf16[4,20,4096]{2,1,0:T(8,128)(2,1)S(1)}, u32[]{:S(2)}, u32[]{:S(2)}) %all-to-all-start.1) | async-done | bytes 655392 | tf_op jit(solution)/shard_map/all_to_all | solution.py:45
  245.6 0.1 reshape.88
  245.8 1.0 fusion.14
  (6 shorter events, 0.1 us)
Async XLA Ops:
  6.5 219.2 %copy-start = (f32[4096,4]{0,1:T(4,128)S(1)}, f32[4096,4]{0,1:T(4,128)}, u32[]{:S(2)}) copy-start(f32[4096,4]{0,1:T(4,128)} %param.7) | copy-start | bytes 196612
  6.5 70.9 %all-gather.2.cloned.1.call-start = ((), (), s32[]{:S(2)}) async-start(), calls=%async_computation.2 | async-start | bytes 5898240 | tf_op jit(solution)/shard_map/all_gather | solution.py:37
  7.8 2.0 copy-start.3
  37.2 181.8 %all-reduce.2.cloned.1.call-start = ((), (), s32[]{:S(2)}) async-start(), calls=%async_computation.3 | async-start | bytes 10485760 | tf_op jit(solution)/shard_map/psum | solution.py:40
  126.5 0.7 copy-start.2
  126.5 99.3 %copy-start.1 = (bf16[32,4096]{1,0:T(8,128)(2,1)S(1)}, bf16[32,4096]{1,0:T(8,128)(2,1)}, u32[]{:S(2)}) copy-start(bf16[32,4096]{1,0:T(8,128)(2,1)} %param.6) | copy-start | bytes 786436
  221.2 24.4 %all-to-all-start.1 = ((bf16[4,20,4096]{2,1,0:T(8,128)(2,1)}), bf16[4,20,4096]{2,1,0:T(8,128)(2,1)S(1)}, u32[]{:S(2)}, u32[]{:S(2)}) async-start(bf16[4,20,4096]{2,1,0:T(8,128)(2,1)} %all_to_all.19), calls=%async_computation.1 | async-start | bytes 1572864 | tf_op jit(solution)/shard_map/all_to_all | solution.py:45
  226.1 1.1 copy-start.4
Sparse Core Ops, SparseCore 0:
  37.3 40.0 all-gather.1
  126.6 92.3 all-reduce.1
where the time goes:
time: 254 us
  waiting for transfers between devices  150 us (59%)
  matrix products  50.6 us (20%)
  blocking collectives  26.3 us (10%)
  between operations  13.5 us (5%)
  local copies, waits for them, and re-layouts  6.75 us (3%)
  starting transfers between devices  4.64 us (2%)
    psum x1, waiting for transfers between devices, on_device(): lax.psum(partial_value.astype(jnp.bfloat16), 'tensor').astype(jnp.float32)  91.7 us
    all_gather x1, waiting for transfers between devices, on_device(): lax.all_gather(arrived, 'tensor', axis=0, tiled=True)  40.2 us
    dot_general x1, matrix products, on_device(): jnp.dot(hidden, weight_down, preferred_element_type=jnp.float32)  33.1 us
    all_to_all x1, blocking collectives, on_device(): lax.all_to_all(buffer, 'expert', split_axis=0, concat_axis=0, tiled=True)  26.3 us
    all_to_all x1, waiting for transfers between devices, on_device(): lax.all_to_all(expert_out, 'expert', split_axis=0, concat_axis=0, tiled=T...  18.3 us
    dot_general x1, matrix products, hidden_units(): jnp.dot(row_piece, weight_gate, preferred_element_type=jnp.float32)  15.9 us
  transfers between devices with their start and end apart: 3, of which 3 were waited for; matrix products, arithmetic and copies ran while one was open for 1% of the time, Pallas kernels for 0%

commit v1 on v0

--- a/solution.py
+++ b/solution.py
@@ -37,7 +37,9 @@
         lax.all_gather(arrived, "tensor", axis=0, tiled=True), weight_gate, weight_up
     )
     partial_value = jnp.dot(hidden, weight_down, preferred_element_type=jnp.float32)
-    summed = lax.psum(partial_value.astype(jnp.bfloat16), "tensor").astype(jnp.float32)
+    summed = jnp.sum(lax.all_gather(partial_value.astype(jnp.bfloat16), "tensor"), axis=0).astype(
+        jnp.float32
+    )
     own_rows = lax.dynamic_slice_in_dim(
         summed, lax.axis_index("tensor") * group_rows, group_rows, 0
     )

time: 254 us -> 376 us (1.48)
  waiting for transfers between devices: 150 us -> 255 us
  other arithmetic: 1.63 us -> 18.7 us
    all_gather x0 -> x1, waiting for transfers between devices: none -> 196 us  [on_device(): lax.all_gather(partial_value.astype(jnp.bfloat16), 'tensor')]
    psum x1 -> x0, waiting for transfers between devices: 91.7 us -> none  [on_device(): lax.psum(partial_value.astype(jnp.bfloat16), 'tensor').astype(jnp.float32)]
    reduce_sum x0 -> x1, other arithmetic: none -> 17.1 us  [on_device(): jnp.sum(lax.all_gather(partial_value.astype(jnp.bfloat16), 'tensor'), axi...]
  transfers between devices with their start and end apart: 3 -> 3, of which waited for: 3 -> 3; matrix products, arithmetic and copies ran while one was open for 1% -> 0% of each run, Pallas kernels for 0% -> 0%
where the time goes in v1:
time: 376 us
  waiting for transfers between devices  255 us (68%)
  matrix products  50.6 us (13%)
  blocking collectives  26.3 us (7%)
  other arithmetic  18.7 us (5%)
  between operations  13.5 us (4%)
  local copies, waits for them, and re-layouts  6.76 us (2%)
  starting transfers between devices  4.64 us (1%)
    all_gather x1, waiting for transfers between devices, on_device(): lax.all_gather(partial_value.astype(jnp.bfloat16), 'tensor')  196 us
    all_gather x1, waiting for transfers between devices, on_device(): lax.all_gather(arrived, 'tensor', axis=0, tiled=True)  40.2 us
    dot_general x1, matrix products, on_device(): jnp.dot(hidden, weight_down, preferred_element_type=jnp.float32)  33.1 us
    all_to_all x1, blocking collectives, on_device(): lax.all_to_all(buffer, 'expert', split_axis=0, concat_axis=0, tiled=True)  26.3 us
    all_to_all x1, waiting for transfers between devices, on_device(): lax.all_to_all(expert_out, 'expert', split_axis=0, concat_axis=0, tiled=T...  18.9 us
    reduce_sum x1, other arithmetic, on_device(): jnp.sum(lax.all_gather(partial_value.astype(jnp.bfloat16), 'tensor'), axi...  17.1 us
    dot_general x1, matrix products, hidden_units(): jnp.dot(row_piece, weight_gate, preferred_element_type=jnp.float32)  15.8 us
  transfers between devices with their start and end apart: 3, of which 3 were waited for; matrix products, arithmetic and copies ran while one was open for 0% of the time, Pallas kernels for 0%

profile of v1, /device:TPU:0, one launch (start us, length us, event | category | flops | bytes accessed | tf_op | source)
XLA Modules:
  0.0 376.0 jit_solution(168362081173735605)
XLA Ops:
  6.5 0.0 copy-start
  6.5 0.0 all-gather.4.cloned.1.call-start
  6.5 0.8 copy.26
  7.3 0.1 reshape.74
  7.4 0.1 fusion.15
  7.5 0.1 reduce_window_sum.11
  7.6 0.2 select_reduce_fusion
  7.8 0.0 copy-start.3
  7.8 1.4 broadcast_in_dim.6
  9.2 0.2 reshape.75
  9.5 0.3 convolution_convert_fusion
  9.8 0.0 copy-done.3
  9.8 0.1 all_to_all.16
  9.9 26.3 %all_to_all.24 = bf16[4,20,4096]{2,1,0:T(8,128)(2,1)S(1)} all-to-all(bf16[4,20,4096]{2,1,0:T(8,128)(2,1)S(1)} %all_to_all.16), channel_id=1, replica_groups=mesh['expert'=4,'tensor'=8] {'expert'}, dimensions={0} | all-to-all | bytes 1310720 | tf_op jit(solution)/shard_map/all_to_all | solution.py:35
  36.2 1.0 all_to_all.18
  37.2 0.0 all-gather.4.cloned.1.call-update
  37.2 0.0 all-gather.6.cloned.1.call-start
  37.3 40.2 %all-gather.4.cloned.1.call-done = bf16[640,4096]{1,0:T(8,128)(2,1)} async-done(((bf16[80,4096]{1,0:T(8,128)(2,1)}), bf16[640,4096]{1,0:T(8,128)(2,1)}) %all-gather.4.cloned.1.call-update) | async-done | bytes 5242896 | tf_op jit(solution)/shard_map/all_gather | solution.py:37
  77.5 15.8 %fusion.4 = f32[640,1792]{1,0:T(8,128)} fusion(bf16[640,4096]{1,0:T(8,128)(2,1)} %all-gather.4.cloned.1.call-done, bf16[1,4096,1792]{2,1,0:T(8,128)(2,1)} %param.9), kind=kOutput, calls=%fused_computation.5 | convolution fusion | flops 9395240960 | bytes 24510464 | tf_op jit(solution)/shard_map/dot_general | solution.py:8
  93.3 33.1 %fusion.6 = bf16[640,4096]{1,0:T(8,128)(2,1)} fusion(bf16[1,1792,4096]{2,1,0:T(8,128)(2,1)} %param.11, f32[640,1792]{1,0:T(8,128)} %fusion.4, bf16[640,4096]{1,0:T(8,128)(2,1)} %all-gather.4.cloned.1.call-done, bf16[1,4096,1792]{2,1,0:T(8,128)(2,1)} %param.10), kind=kOutput, calls=%fused_computation.7 | convolution fusion | flops 18799984640 | bytes 44433408 | tf_op jit(solution)/shard_map/dot_general | solution.py:39
  126.4 0.0 copy-start.2
  126.4 0.0 all-gather.6.cloned.1.call-update
  126.4 0.6 copy-done.2
  127.1 0.1 copy.28
  127.2 0.1 reshape.77
  127.3 196.3 %all-gather.6.cloned.1.call-done = bf16[5120,4096]{1,0:T(8,128)(2,1)} async-done(((bf16[640,4096]{1,0:T(8,128)(2,1)}), bf16[5120,4096]{1,0:T(8,128)(2,1)}) %all-gather.6.cloned.1.call-update) | async-done | bytes 41943056 | tf_op jit(solution)/shard_map/all_gather | solution.py:40
  323.6 0.0 copy-start.1
  323.6 17.1 %reduce_sum.40 = bf16[640,4096]{1,0:T(8,128)(2,1)} reduce(bf16[8,640,4096]{2,1,0:T(8,128)(2,1)} %bitcast.26, bf16[]{:T(256)} %constant.21.clone.1), dimensions={0}, to_apply=%region_2.3 | reduce | flops 18350080 | bytes 47185920 | tf_op jit(solution)/shard_map/reduce_sum | solution.py:40
  340.7 1.1 convert_convert_fusion
  341.8 1.0 all_to_all.19
  342.9 4.6 %all-to-all-start.1 = ((bf16[4,20,4096]{2,1,0:T(8,128)(2,1)}), bf16[4,20,4096]{2,1,0:T(8,128)(2,1)S(1)}, u32[]{:S(2)}, u32[]{:S(2)}) async-start(bf16[4,20,4096]{2,1,0:T(8,128)(2,1)} %all_to_all.19), calls=%async_computation.1 | async-start | bytes 1572864 | tf_op jit(solution)/shard_map/all_to_all | solution.py:47
  347.5 0.0 copy-done
  347.5 0.0 copy-done.1
  347.5 0.3 fusion.22
  347.8 0.0 copy-start.4
  347.8 0.9 gather_fusion
  348.7 0.1 reshape.80
  348.8 0.1 copy.29
  348.8 0.0 copy-done.4
  348.9 0.1 iota_compare_fusion.3
  349.0 18.9 %all-to-all-done.1 = bf16[4,20,4096]{2,1,0:T(8,128)(2,1)S(1)} async-done(((bf16[4,20,4096]{2,1,0:T(8,128)(2,1)}), bf16[4,20,4096]{2,1,0:T(8,128)(2,1)S(1)}, u32[]{:S(2)}, u32[]{:S(2)}) %all-to-all-start.1) | async-done | bytes 655392 | tf_op jit(solution)/shard_map/all_to_all | solution.py:47
  368.0 0.1 reshape.89
  368.1 1.0 fusion.14
  (6 shorter events, 0.1 us)
Async XLA Ops:
  6.5 340.9 %copy-start = (f32[4096,4]{0,1:T(4,128)S(1)}, f32[4096,4]{0,1:T(4,128)}, u32[]{:S(2)}) copy-start(f32[4096,4]{0,1:T(4,128)} %param.7) | copy-start | bytes 196612
  6.5 70.9 %all-gather.4.cloned.1.call-start = ((), (), s32[]{:S(2)}) async-start(), calls=%async_computation.2 | async-start | bytes 5898240 | tf_op jit(solution)/shard_map/all_gather | solution.py:37
  7.8 2.0 copy-start.3
  37.2 286.4 %all-gather.6.cloned.1.call-start = ((), (), s32[]{:S(2)}) async-start(), calls=%async_computation.3 | async-start | bytes 47185920 | tf_op jit(solution)/shard_map/all_gather | solution.py:40
  126.4 0.7 copy-start.2
  323.6 23.9 %copy-start.1 = (bf16[32,4096]{1,0:T(8,128)(2,1)S(1)}, bf16[32,4096]{1,0:T(8,128)(2,1)}, u32[]{:S(2)}) copy-start(bf16[32,4096]{1,0:T(8,128)(2,1)} %param.6) | copy-start | bytes 786436
  342.9 25.1 %all-to-all-start.1 = ((bf16[4,20,4096]{2,1,0:T(8,128)(2,1)}), bf16[4,20,4096]{2,1,0:T(8,128)(2,1)S(1)}, u32[]{:S(2)}, u32[]{:S(2)}) async-start(bf16[4,20,4096]{2,1,0:T(8,128)(2,1)} %all_to_all.19), calls=%async_computation.1 | async-start | bytes 1572864 | tf_op jit(solution)/shard_map/all_to_all | solution.py:47
  347.8 1.1 copy-start.4
Sparse Core Ops, SparseCore 0:
  37.3 40.0 all-gather.3
  126.6 196.9 all-gather.5
